TPU v7x, 32 devices: a whole 2x2x4 slice. The times are simulated.
32 devices in a mesh: row: 4 (over y, x), col: 4 (over z), img: 2 (over core).
Axes of the slice: x: 2, y: 2, z: 4, core: 2. Of those that a mesh axis runs over, the one named last changes fastest.
Arguments:
- student: bfloat16 [2, 1024, 4096], P('img', 'col', 'row'), may hold values from -6 to 6
- teacher: bfloat16 [2, 1024, 4096], P('img', 'col', 'row'), may hold values from -6 to 6
Outputs:
- feature_grad: bfloat16 [2, 1024, 4096], P('img', 'col', 'row')
All inputs are finite; a program needn't handle non-finite values.
Results may differ from a plain program's by a relative error of at most 0.012.
Values may be sent and summed in bfloat16 or wider, within the bound.
No kernel may reach another device: no remote copies, remote signals or barrier semaphores. Data moves between devices by JAX's collectives and lax.ppermute only.
A program may use at most 64 MiB of HBM per device.

v0:
```python
import jax
import jax.numpy as jnp
from jax import lax
from jax.sharding import PartitionSpec as P


def body(student, teacher):
    width = student.shape[2] * lax.axis_size("row")
    own_student, own_teacher = (
        lax.all_gather(student, "row", axis=2, tiled=True),
        lax.all_gather(teacher, "row", axis=2, tiled=True),
    )
    band_student, band_teacher = (
        lax.all_gather(student, "col", axis=1, tiled=True),
        lax.all_gather(teacher, "col", axis=1, tiled=True),
    )
    row_student, row_teacher = (
        lax.all_to_all(band_student, "row", split_axis=1, concat_axis=2, tiled=True),
        lax.all_to_all(band_teacher, "row", split_axis=1, concat_axis=2, tiled=True),
    )
    gram_student = jnp.einsum(
        "ipd,iqd->ipq", row_student, own_student, preferred_element_type=jnp.float32
    )
    gram_teacher = jnp.einsum(
        "ipd,iqd->ipq", row_teacher, own_teacher, preferred_element_type=jnp.float32
    )
    gap = ((gram_student - gram_teacher) / width).astype(jnp.bfloat16)
    partial_term = jnp.einsum("ipq,ipd->iqd", gap, row_student, preferred_element_type=jnp.float32)
    summed = lax.psum_scatter(
        partial_term.astype(jnp.bfloat16), "row", scatter_dimension=2, tiled=True
    )
    return summed


def solution(mesh):
    placed = (P("img", "col", "row"), P("img", "col", "row"))
    return jax.shard_map(
        body, mesh=mesh, in_specs=placed, out_specs=P("img", "col", "row"), check_vma=False
    )
```

profile of v0, /device:TPU:0, one launch (start us, length us, event | category | flops | bytes accessed | tf_op | source)
XLA Modules:
  0.0 238.9 jit_solution(11923365194114167094)
XLA Ops:
  6.5 0.0 all-gather.9.cloned.1.call-start
  6.5 0.7 all-gather.9.cloned.1.call-update
  7.3 0.0 all-gather.5.cloned.1.call-start
  7.3 0.7 all-gather.5.cloned.1.call-update
  8.0 0.0 all-gather.11.cloned.1.call-start
  8.1 0.7 all-gather.11.cloned.1.call-update
  8.7 48.6 %all-gather.9.cloned.1.call-done = bf16[1,1024,1024]{2,1,0:T(8,128)(2,1)} async-done(((bf16[1,256,1024]{2,1,0:T(8,128)(2,1)}), bf16[1,1024,1024]{2,1,0:T(8,128)(2,1)}) %all-gather.9.cloned.1.call-update) | async-done | bytes 2097168 | tf_op jit(solution)/shard_map/all_gather | solution.py:15
  57.3 6.8 %copy.17 = bf16[1,1024,1024]{2,0,1:T(2,128)(2,1)} copy(bf16[1,1024,1024]{2,1,0:T(8,128)(2,1)} %all-gather.9.cloned.1.call-done) | data formatting | bytes 4194304 | tf_op jit(solution)/shard_map/all_gather | solution.py:15
  64.1 0.5 broadcast.2
  64.6 12.8 %reduce.1 = bf16[1024,1024]{1,0:T(8,128)(2,1)S(1)} reduce(bf16[1024,1,1024]{2,1,0:T(2,128)(2,1)} %bitcast.36, bf16[]{:T(256)} %broadcast.2), dimensions={1}, to_apply=%bitcast.33.reduce_sub_computation | reduce | bytes 4194306
  77.4 2.8 %reshape.31 = bf16[4,2,131072]{2,1,0:T(2,128)(2,1)} reshape(bf16[1024,1024]{1,0:T(8,128)(2,1)S(1)} %reduce.1) | data formatting | bytes 4194304
  80.2 3.6 %all-to-all-start.1 = ((bf16[4,2,131072]{2,1,0:T(2,128)(2,1)}), bf16[4,2,131072]{2,1,0:T(2,128)(2,1)S(1)}, u32[]{:S(2)}, u32[]{:S(2)}) async-start(bf16[4,2,131072]{2,1,0:T(2,128)(2,1)} %reshape.31), calls=%async_computation.1 | async-start | bytes 4194304 | tf_op jit(solution)/shard_map/all_to_all | solution.py:19
  83.9 0.2 all-gather.7.cloned.1.call-start
  84.1 0.3 all-gather.7.cloned.1.call-update
  84.4 18.9 %all-gather.5.cloned.1.call-done = bf16[1,1024,1024]{2,1,0:T(8,128)(2,1)} async-done(((bf16[1,256,1024]{2,1,0:T(8,128)(2,1)}), bf16[1,1024,1024]{2,1,0:T(8,128)(2,1)}) %all-gather.5.cloned.1.call-update) | async-done | bytes 2097168 | tf_op jit(solution)/shard_map/all_gather | solution.py:14
  103.4 6.8 %copy.18 = bf16[1,1024,1024]{2,0,1:T(2,128)(2,1)} copy(bf16[1,1024,1024]{2,1,0:T(8,128)(2,1)} %all-gather.5.cloned.1.call-done) | data formatting | bytes 4194304 | tf_op jit(solution)/shard_map/all_gather | solution.py:14
  110.1 14.2 %reduce = bf16[1024,1024]{1,0:T(8,128)(2,1)} reduce(bf16[1024,1,1024]{2,1,0:T(2,128)(2,1)} %bitcast.37, bf16[]{:T(256)} %broadcast.2), dimensions={1}, to_apply=%bitcast.34.reduce_sub_computation | reduce | bytes 4194306
  124.3 4.5 %reshape.29 = bf16[4,2,131072]{2,1,0:T(2,128)(2,1)} reshape(bf16[1024,1024]{1,0:T(8,128)(2,1)} %reduce) | data formatting | bytes 4194304
  128.8 0.0 all-to-all-done.1
  128.8 4.5 %all-to-all-start = ((bf16[4,2,131072]{2,1,0:T(2,128)(2,1)}), bf16[4,2,131072]{2,1,0:T(2,128)(2,1)}, u32[]{:S(2)}, u32[]{:S(2)}) async-start(bf16[4,2,131072]{2,1,0:T(2,128)(2,1)} %reshape.29), calls=%async_computation | async-start | bytes 4194304 | tf_op jit(solution)/shard_map/all_to_all | solution.py:18
  133.3 0.3 reduce-scatter.2.cloned.1.call-start
  133.6 3.4 %reshape.32 = bf16[1024,1,1024]{2,1,0:T(2,128)(2,1)} reshape(bf16[4,2,131072]{2,1,0:T(2,128)(2,1)S(1)} %all-to-all-done.1) | data formatting | bytes 4194304
  136.9 3.0 %copy.14 = bf16[1,1024,1024]{2,1,0:T(8,128)(2,1)S(1)} copy(bf16[1,1024,1024]{2,0,1:T(2,128)(2,1)} %bitcast.38) | data formatting | bytes 4194304
  139.9 2.6 %copy.12 = bf16[1,256,4,1024]{1,3,2,0:T(8,128)(2,1)} copy(bf16[1,256,4,1024]{3,1,2,0:T(8,128)(2,1)S(1)} %bitcast.40) | data formatting | bytes 4194304 | tf_op jit(solution)/shard_map/all_to_all | solution.py:19
  142.6 19.0 %all-to-all-done = bf16[4,2,131072]{2,1,0:T(2,128)(2,1)} async-done(((bf16[4,2,131072]{2,1,0:T(2,128)(2,1)}), bf16[4,2,131072]{2,1,0:T(2,128)(2,1)}, u32[]{:S(2)}, u32[]{:S(2)}) %all-to-all-start) | async-done | bytes 2097184 | tf_op jit(solution)/shard_map/all_to_all | solution.py:18
  161.5 5.0 %reshape.30 = bf16[1024,1,1024]{2,1,0:T(2,128)(2,1)} reshape(bf16[4,2,131072]{2,1,0:T(2,128)(2,1)} %all-to-all-done) | data formatting | bytes 4194304
  166.5 4.3 %copy.13 = bf16[1,1024,1024]{2,1,0:T(8,128)(2,1)} copy(bf16[1,1024,1024]{2,0,1:T(2,128)(2,1)} %bitcast.39) | data formatting | bytes 4194304
  170.8 2.8 %copy.10 = bf16[1,256,4,1024]{1,3,2,0:T(8,128)(2,1)S(1)} copy(bf16[1,256,4,1024]{3,1,2,0:T(8,128)(2,1)} %bitcast.41) | data formatting | bytes 4194304 | tf_op jit(solution)/shard_map/all_to_all | solution.py:18
  173.7 0.0 all-gather.11.cloned.1.call-done
  173.7 3.0 %fusion.1 = f32[256,256]{1,0:T(8,128)S(1)} fusion(bf16[256,4096]{0,1:T(8,128)(2,1)} %bitcast.42, bf16[1,256,4096]{2,1,0:T(8,128)(2,1)} %all-gather.11.cloned.1.call-done), kind=kOutput, calls=%fused_computation.2 | convolution fusion | flops 536870912 | bytes 4456448 | tf_op jit(solution)/shard_map/ipd,iqd->ipq/dot_general | solution.py:24
  176.7 14.9 %all-gather.7.cloned.1.call-done = bf16[1,256,4096]{2,1,0:T(8,128)(2,1)} async-done(((bf16[1,256,1024]{2,1,0:T(8,128)(2,1)}), bf16[1,256,4096]{2,1,0:T(8,128)(2,1)}) %all-gather.7.cloned.1.call-update) | async-done | bytes 2097168 | tf_op jit(solution)/shard_map/all_gather | solution.py:10
  191.6 5.4 %fusion = bf16[1,256,4096]{2,1,0:T(8,128)(2,1)} fusion(bf16[256,4096]{0,1:T(8,128)(2,1)S(1)} %bitcast.35, f32[256,256]{1,0:T(8,128)S(1)} %fusion.1, bf16[1,256,4096]{2,1,0:T(8,128)(2,1)} %all-gather.7.cloned.1.call-done), kind=kOutput, calls=%fused_computation.1 | convolution fusion | flops 1074987008 | bytes 6553600 | tf_op jit(solution)/shard_map/ipq,ipd->iqd/dot_general | solution.py:28
  197.0 0.0 reduce-scatter.2.cloned.1.call-update
  197.1 35.3 %reduce-scatter.2.cloned.1.call-done = bf16[1,256,1024]{2,1,0:T(8,128)(2,1)} async-done(((bf16[1,256,4096]{2,1,0:T(8,128)(2,1)}), bf16[1,256,1024]{2,1,0:T(8,128)(2,1)}) %reduce-scatter.2.cloned.1.call-update) | async-done | bytes 524304 | tf_op jit(solution)/shard_map/reduce_scatter | solution.py:29
Async XLA Ops:
  6.5 50.8 %all-gather.9.cloned.1.call-start = ((), (), s32[]{:S(2)}) async-start(), calls=%async_computation.5 | async-start | bytes 2621440 | tf_op jit(solution)/shard_map/all_gather | solution.py:15
  7.3 96.1 %all-gather.5.cloned.1.call-start = ((), (), s32[]{:S(2)}) async-start(), calls=%async_computation.3 | async-start | bytes 2621440 | tf_op jit(solution)/shard_map/all_gather | solution.py:14
  8.0 165.7 %all-gather.11.cloned.1.call-start = ((), (), s32[]{:S(2)}) async-start(), calls=%async_computation.6 | async-start | bytes 2621440 | tf_op jit(solution)/shard_map/all_gather | solution.py:11
  80.2 48.6 %all-to-all-start.1 = ((bf16[4,2,131072]{2,1,0:T(2,128)(2,1)}), bf16[4,2,131072]{2,1,0:T(2,128)(2,1)S(1)}, u32[]{:S(2)}, u32[]{:S(2)}) async-start(bf16[4,2,131072]{2,1,0:T(2,128)(2,1)} %reshape.31), calls=%async_computation.1 | async-start | bytes 4194304 | tf_op jit(solution)/shard_map/all_to_all | solution.py:19
  83.9 107.7 %all-gather.7.cloned.1.call-start = ((), (), s32[]{:S(2)}) async-start(), calls=%async_computation.4 | async-start | bytes 2621440 | tf_op jit(solution)/shard_map/all_gather | solution.py:10
  128.8 32.7 %all-to-all-start = ((bf16[4,2,131072]{2,1,0:T(2,128)(2,1)}), bf16[4,2,131072]{2,1,0:T(2,128)(2,1)}, u32[]{:S(2)}, u32[]{:S(2)}) async-start(bf16[4,2,131072]{2,1,0:T(2,128)(2,1)} %reshape.29), calls=%async_computation | async-start | bytes 4194304 | tf_op jit(solution)/shard_map/all_to_all | solution.py:18
  133.3 99.1 %reduce-scatter.2.cloned.1.call-start = ((), (), s32[]{:S(2)}) async-start(), calls=%async_computation.7 | async-start | bytes 2621440 | tf_op jit(solution)/shard_map/reduce_scatter | solution.py:29
Sparse Core Ops, SparseCore 0:
  8.9 48.3 all-gather.8
  58.9 44.4 all-gather.4
  105.2 48.2 all-gather.10
  155.2 36.3 all-gather.6
  197.2 35.1 reduce-scatter.1
where the time goes:
time: 240 us; the launch traced here: 239 us
  waiting for transfers between devices  139 us (58%)
  local copies, waits for them, and re-layouts  42.5 us (18%)
  other arithmetic  27 us (11%)
  between operations  13.2 us (6%)
  starting transfers between devices  8.64 us (4%)
  matrix products  8.42 us (4%)
    all_gather x1, waiting for transfers between devices, body(): lax.all_gather(teacher, 'col', axis=1, tiled=True)  48.6 us
    reduce_scatter x1, waiting for transfers between devices, body(): lax.psum_scatter(partial_term.astype(jnp.bfloat16), 'row', scatter_dimens...  35.3 us
    unnamed x2, other arithmetic  27 us
    unnamed x7, local copies, waits for them, and re-layouts  23.5 us
    all_to_all x1, waiting for transfers between devices, body(): lax.all_to_all(band_student, 'row', split_axis=1, concat_axis=2, tiled=True)  19 us
    all_gather x1, waiting for transfers between devices, body(): lax.all_gather(student, 'col', axis=1, tiled=True)  18.9 us
    all_gather x1, waiting for transfers between devices, body(): lax.all_gather(student, 'row', axis=2, tiled=True)  14.9 us
    all_gather x1, local copies, waits for them, and re-layouts, body(): lax.all_gather(teacher, 'col', axis=1, tiled=True)  6.77 us
  transfers between devices with their start and end apart: 7, of which 5 were waited for; matrix products, arithmetic and copies ran while one was open for 30% of the time, Pallas kernels for 0%

commit v1 on v0

v1 whole, which is shorter than its diff:
```python
import functools

import jax
import jax.numpy as jnp
from jax import lax
from jax.experimental import pallas as pl
from jax.experimental.pallas import tpu as pltpu
from jax.sharding import PartitionSpec as P

AXES = ("row", "col", "img")
NT = (((1,), (1,)), ((), ()))
NN = (((1,), (0,)), ((), ()))
TN = (((0,), (0,)), ((), ()))
VMEM = pltpu.MemorySpace.VMEM


def dot(a, b, dims):
    return lax.dot_general(a, b, dims, preferred_element_type=jnp.float32)


def place(n_col):
    col = lax.axis_index("col")
    return jnp.where(lax.axis_index("img") % 2 == 1, n_col - 1 - col, col)


def gram_kernel(pairs, n_row, names, *refs):
    count = len(names)
    s = dict(zip(names, refs[:count]))
    t = dict(zip(names, refs[count : 2 * count]))
    outs, block = refs[2 * count : -1], refs[-1]
    me = lax.axis_index("row")
    rows = block.shape[0] // n_row
    for at, (i, j) in enumerate(pairs):
        block[...] = dot(s[i][...], s[j][...], NT) - dot(t[i][...], t[j][...], NT)
        for k, out in enumerate(outs):
            start = pl.multiple_of((me ^ k) * rows, rows)
            out[at] = block[pl.ds(start, rows), :].astype(out.dtype)


def gram(pairs, n_row, s, t):
    names = tuple(sorted(s))
    size, depth = s[names[0]].shape
    shape = jax.ShapeDtypeStruct((len(pairs), size // n_row, size), jnp.bfloat16)
    flops = 4 * len(pairs) * size * size * depth
    moved = 2 * (2 * len(names) * size * depth + len(pairs) * size * size)
    return pl.pallas_call(
        functools.partial(gram_kernel, pairs, n_row, names),
        out_shape=[shape] * n_row,
        in_specs=[pl.BlockSpec(memory_space=VMEM)] * (2 * len(names)),
        out_specs=[pl.BlockSpec(memory_space=VMEM)] * n_row,
        scratch_shapes=[pltpu.VMEM((size, size), jnp.float32)],
        cost_estimate=pl.CostEstimate(flops=flops, bytes_accessed=moved, transcendentals=0),
    )(*[s[i] for i in names], *[t[i] for i in names])


def sum_kernel(n_col, n_row, width, chunks, *refs):
    outs = refs[-n_col:]
    at = 0
    for pairs in chunks:
        group = refs[at : at + n_row]
        at += n_row
        for b, (i, j) in enumerate(pairs):
            total = group[0][b].astype(jnp.float32)
            for other in group[1:]:
                total += other[b].astype(jnp.float32)
            total = (total / width).astype(jnp.bfloat16)
            outs[i][j] = total
            if i != j:
                outs[j][i] = total


def add_up(n_col, n_row, width, chunks, parts):
    rows, size = parts[0].shape[1:]
    shape = jax.ShapeDtypeStruct((n_col, rows, size), jnp.bfloat16)
    count = sum(len(pairs) for pairs in chunks)
    return pl.pallas_call(
        functools.partial(sum_kernel, n_col, n_row, width, chunks),
        out_shape=[shape] * n_col,
        in_specs=[pl.BlockSpec(memory_space=VMEM)] * len(parts),
        out_specs=[pl.BlockSpec(memory_space=VMEM)] * n_col,
        cost_estimate=pl.CostEstimate(
            flops=n_row * count * rows * size,
            bytes_accessed=2 * (n_row * count + n_col * n_col) * rows * size,
            transcendentals=0,
        ),
    )(*parts)


def final_kernel(n_col, n_row, *refs):
    gaps, own, rest = refs[:n_row], refs[n_row], refs[n_row + 1 : -3]
    lefts, rights = rest[: n_col - 1], rest[n_col - 1 :]
    out, block, total = refs[-3:]
    me, z = lax.axis_index("row"), place(n_col)
    rows = gaps[0].shape[1]

    def load(at):
        for k, gap in enumerate(gaps):
            start = pl.multiple_of((me ^ k) * rows, rows)
            block[pl.ds(start, rows), :] = gap[at]

    load(z)
    total[...] = dot(block[...], own[...], NN)
    for k in range(1, n_col):

        @pl.when(z + k < n_col)
        def _():
            load(z + k)
            total[...] += dot(block[...], lefts[k - 1][...], TN)

        @pl.when(z - k >= 0)
        def _():
            load(z - k)
            total[...] += dot(block[...], rights[k - 1][...], NN)

    out[...] = total[...].astype(out.dtype)


def finish(n_col, n_row, gaps, own, lefts, rights):
    size, depth = own.shape
    args = (*gaps, own, *lefts, *rights)
    return pl.pallas_call(
        functools.partial(final_kernel, n_col, n_row),
        out_shape=jax.ShapeDtypeStruct((size, depth), jnp.bfloat16),
        in_specs=[pl.BlockSpec(memory_space=VMEM)] * len(args),
        out_specs=pl.BlockSpec(memory_space=VMEM),
        scratch_shapes=[pltpu.VMEM((size, size), jnp.bfloat16), pltpu.VMEM((size, depth), jnp.float32)],
        cost_estimate=pl.CostEstimate(
            flops=2 * n_col * size * size * depth,
            bytes_accessed=2 * (2 * n_col * size * depth + n_col * size * size),
            transcendentals=0,
        ),
    )(*args)


def body(student, teacher):
    n_row, n_col, n_img = (lax.axis_size(a) for a in AXES)
    width = student.shape[2] * n_row
    own_s = student.reshape(student.shape[1:])
    own_t = teacher.reshape(teacher.shape[1:])
    hub, last = n_col // 2 - 1, n_col - 1
    z = place(n_col)

    def index(row, at, img):
        col = n_col - 1 - at if img % 2 else at
        return (row * n_col + col) * n_img + img

    def along_col(x, pairs):
        perm = [
            (index(r, a, g), index(r, b, g)) for r in range(n_row) for g in range(n_img) for a, b in pairs
        ]
        return lax.ppermute(x, AXES, perm)

    def along_row(x, k, places):
        perm = [
            (index(r, a, g), index(r ^ k, a, g)) for r in range(n_row) for g in range(n_img) for a in places
        ]
        return lax.ppermute(x, AXES, perm)

    t, s = {hub: own_t}, {hub: own_s}
    for p in range(last, hub, -1):
        t[p] = along_col(own_t, [(p, hub)])
    lefts = [along_col(own_s, [(i + 1, i) for i in range(last)])]
    held_s, held_t, _ = lax.optimization_barrier((own_s, own_t, lefts[0]))
    for p in range(hub):
        t[p] = along_col(held_t, [(p, hub)])
    early, x = [], held_s
    for k in range(1, hub + 1):
        x = along_col(x, [(i, i + 1) for i in range(k - 1, hub)])
        early.append(x)
        s[hub - k] = x
    s[hub + 1] = lefts[0]
    for k in range(2, n_col - hub):
        lefts.append(along_col(lefts[-1], [(i + 1, i) for i in range(n_col - k)]))
        s[hub + k] = lefts[-1]

    pairs_a = tuple((i, j) for i in range(last) for j in range(i + 1))
    pairs_b = tuple((last, j) for j in range(n_col))
    parts = []
    for pairs in (pairs_a, pairs_b):
        used = {p for pair in pairs for p in pair}
        sent = gram(pairs, n_row, {p: s[p] for p in used}, {p: t[p] for p in used})
        parts.append(sent[0])
        parts.extend(along_row(sent[k], k, (hub,)) for k in range(1, n_row))

    late_s, *_ = lax.optimization_barrier((own_s, lefts[-1], t[0]))
    for k in range(n_col - hub, n_col):
        lefts.append(along_col(lefts[-1], [(i + 1, i) for i in range(n_col - k)]))
    rights, x = [], late_s
    for k in range(1, n_col):
        x = along_col(x, [(i, i + 1) for i in range(max(hub, k - 1), last)])
        if k <= hub:
            x = x + early[k - 1]
        rights.append(x)

    quarters = add_up(n_col, n_row, width, (pairs_a, pairs_b), parts)
    mine = jnp.where(z == hub, quarters[hub], jnp.zeros_like(quarters[hub]))
    for p in range(n_col):
        if p != hub:
            mine = mine + along_col(quarters[p], [(hub, p)])
    gaps = [mine] + [along_row(mine, k, range(n_col)) for k in range(1, n_row)]
    out = finish(n_col, n_row, gaps, own_s, lefts, rights)
    return out.reshape(student.shape)


def solution(mesh):
    placed = (P("img", "col", "row"), P("img", "col", "row"))
    return jax.shard_map(
        body, mesh=mesh, in_specs=placed, out_specs=P("img", "col", "row"), check_vma=False
    )
```

time: 240 us -> 109 us (0.45)
  waiting for transfers between devices: 139 us -> 61.8 us
  local copies, waits for them, and re-layouts: 42.5 us -> 3.02 us
  other arithmetic: 27 us -> 0.22 us
  starting transfers between devices: 8.64 us -> 27.7 us
  Pallas kernels: 0 us -> 15.7 us
  between operations: 13.2 us -> 0.43 us
  matrix products: 8.42 us -> 0 us
    all_gather x4 -> x0, waiting for transfers between devices: 82.4 us -> none  [the longest x1 48.6 us: body(): lax.all_gather(teacher, 'col', axis=1, tiled=True)]
    ppermute x0 -> x22, waiting for transfers between devices: none -> 61.8 us  [the longest x13 57.3 us: along_col(): return lax.ppermute(x, AXES, perm)]
    reduce_scatter x1 -> x0, waiting for transfers between devices: 35.3 us -> none  [body(): lax.psum_scatter(partial_term.astype(jnp.bfloat16), 'row', scatter_dimens...]
    ppermute x0 -> x22, starting transfers between devices: none -> 27.7 us  [the longest x13 20 us: along_col(): return lax.ppermute(x, AXES, perm)]
    unnamed x2 -> x0, other arithmetic: 27 us -> none
    unnamed x7 -> x40, local copies, waits for them, and re-layouts: 23.5 us -> 3.02 us
    all_to_all x2 -> x0, waiting for transfers between devices: 19 us -> none  [the longest x1 19 us: body(): lax.all_to_all(band_student, 'row', split_axis=1, concat_axis=2, tiled=True)]
    pallas_call x0 -> x4, Pallas kernels: none -> 15.7 us  [the longest x2 9.07 us: gram(): pl.pallas_call(functools.partial(gram_kernel, pairs, n_row, names), out_s...]
  transfers between devices with their start and end apart: 7 -> 22, of which waited for: 5 -> 7; matrix products, arithmetic and copies ran while one was open for 30% -> 0% of each run, Pallas kernels for 0% -> 10%
where the time goes in v1:
time: 109 us
  waiting for transfers between devices  61.8 us (57%)
  starting transfers between devices  27.7 us (25%)
  Pallas kernels  15.7 us (14%)
  local copies, waits for them, and re-layouts  3.02 us (3%)
    ppermute x13, waiting for transfers between devices, along_col(): return lax.ppermute(x, AXES, perm)  57.3 us
    ppermute x13, starting transfers between devices, along_col(): return lax.ppermute(x, AXES, perm)  20 us
    pallas_call x2, Pallas kernels, gram(): pl.pallas_call(functools.partial(gram_kernel, pairs, n_row, names), out_s...  9.07 us
    ppermute x9, starting transfers between devices, along_row(): return lax.ppermute(x, AXES, perm)  7.69 us
    ppermute x9, waiting for transfers between devices, along_row(): return lax.ppermute(x, AXES, perm)  4.46 us
    pallas_call x1, Pallas kernels, finish(): pl.pallas_call(functools.partial(final_kernel, n_col, n_row), out_shape=j...  4.35 us
    unnamed x40, local copies, waits for them, and re-layouts  3.02 us
    pallas_call x1, Pallas kernels, add_up(): pl.pallas_call(functools.partial(sum_kernel, n_col, n_row, width, chunks)...  2.26 us
  transfers between devices with their start and end apart: 22, of which 7 were waited for; matrix products, arithmetic and copies ran while one was open for 0% of the time, Pallas kernels for 10%

profile of v1, /device:TPU:0, one launch (start us, length us, event | category | flops | bytes accessed | tf_op | source)
XLA Modules:
  0.0 108.9 jit_solution(16083401560634926282)
XLA Ops:
  0.0 1.3 %collective-permute-start = (bf16[256,1024]{1,0:T(8,128)(2,1)}, bf16[256,1024]{1,0:T(8,128)(2,1)S(1)}, u32[]{:S(2)}, u32[]{:S(2)}) collective-permute-start(bf16[256,1024]{1,0:T(8,128)(2,1)} %bitcast.3), channel_id=1, source_target_pairs={{2,0},{4,2},{6,4},{5,7},{3,5},{1,3},{10,8},{12,10},{14,12},{13,15}... | collective-permute-start | bytes 1572872 | tf_op jit(solution)/shard_map/ppermute | solution.py:151
  1.3 11.0 %collective-permute-done.refs_2_.refs_5_ = bf16[256,1024]{1,0:T(8,128)(2,1)S(1)} collective-permute-done((bf16[256,1024]{1,0:T(8,128)(2,1)}, bf16[256,1024]{1,0:T(8,128)(2,1)S(1)}, u32[]{:S(2)}, u32[]{:S(2)}) %collective-permute-start) | collective-permute-done | bytes 524320 | tf_op jit(solution)/shard_map/ppermute | solution.py:151
  12.3 3.9 %collective-permute-start.2 = (bf16[256,1024]{1,0:T(8,128)(2,1)}, bf16[256,1024]{1,0:T(8,128)(2,1)S(1)}, u32[]{:S(2)}, u32[]{:S(2)}) collective-permute-start(bf16[256,1024]{1,0:T(8,128)(2,1)} %bitcast.9), channel_id=1, source_target_pairs={{0,2},{7,5},{8,10},{15,13},{16,18},{23,21},{24,26},{31,29}} | collective-permute-start | bytes 1572872 | tf_op jit(solution)/shard_map/ppermute | solution.py:151
  16.3 1.3 %collective-permute-start.7 = (bf16[256,1024]{1,0:T(8,128)(2,1)S(1)}, bf16[256,1024]{1,0:T(8,128)(2,1)S(1)}, u32[]{:S(2)}, u32[]{:S(2)}) collective-permute-start(bf16[256,1024]{1,0:T(8,128)(2,1)S(1)} %collective-permute-done.refs_2_.refs_5_), channel_id=1, source_target_pairs={{2,0},{4,2},{5,7},{3,5},{10,8},{12,10},{13,15},{11,13},{18,16},{20... | collective-permute-start | bytes 1572872 | tf_op jit(solution)/shard_map/ppermute | solution.py:151
  17.6 4.6 %collective-permute-start.1 = (bf16[256,1024]{1,0:T(8,128)(2,1)}, bf16[256,1024]{1,0:T(8,128)(2,1)S(1)}, u32[]{:S(2)}, u32[]{:S(2)}) collective-permute-start(bf16[256,1024]{1,0:T(8,128)(2,1)} %bitcast.4), channel_id=1, source_target_pairs={{0,2},{7,5},{8,10},{15,13},{16,18},{23,21},{24,26},{31,29}} | collective-permute-start | bytes 1572872 | tf_op jit(solution)/shard_map/ppermute | solution.py:151
  22.2 1.1 collective-permute-done.2.refs_3_.refs_4_
  23.2 4.6 %collective-permute-done.7.refs_3_.refs_6_ = bf16[256,1024]{1,0:T(8,128)(2,1)S(1)} collective-permute-done((bf16[256,1024]{1,0:T(8,128)(2,1)S(1)}, bf16[256,1024]{1,0:T(8,128)(2,1)S(1)}, u32[]{:S(2)}, u32[]{:S(2)}) %collective-permute-start.7) | collective-permute-done | bytes 524320 | tf_op jit(solution)/shard_map/ppermute | solution.py:151
  27.8 0.7 collective-permute-start.19
  28.5 1.5 %collective-permute-start.3 = (bf16[256,1024]{1,0:T(8,128)(2,1)}, bf16[256,1024]{1,0:T(8,128)(2,1)}, u32[]{:S(2)}, u32[]{:S(2)}) collective-permute-start(bf16[256,1024]{1,0:T(8,128)(2,1)} %bitcast.10), channel_id=1, source_target_pairs={{4,2},{3,5},{12,10},{11,13},{20,18},{19,21},{28,26},{27,29}} | collective-permute-start | bytes 1572872 | tf_op jit(solution)/shard_map/ppermute | solution.py:151
  30.0 1.5 %collective-permute-start.8 = (bf16[256,1024]{1,0:T(8,128)(2,1)}, bf16[256,1024]{1,0:T(8,128)(2,1)}, u32[]{:S(2)}, u32[]{:S(2)}) collective-permute-start(bf16[256,1024]{1,0:T(8,128)(2,1)} %bitcast.11), channel_id=1, source_target_pairs={{6,2},{1,5},{14,10},{9,13},{22,18},{17,21},{30,26},{25,29}} | collective-permute-start | bytes 1572872 | tf_op jit(solution)/shard_map/ppermute | solution.py:151
  31.5 0.0 collective-permute-done.1.refs_0_
  31.5 0.0 collective-permute-done.19
  31.5 0.2 add.20.refs_8_
  31.7 0.0 copy-done.1
  31.7 0.0 copy-done.2
  31.7 0.6 copy-done.4
  32.3 0.7 collective-permute-start.20
  32.9 0.0 collective-permute-done.3.refs_5_.refs_6_
  33.0 0.0 collective-permute-done.8.refs_7_
  33.0 0.0 copy-done.9
  33.0 4.3 %shard_map.29 = (bf16[4,64,256]{2,1,0:T(8,128)(2,1)}, bf16[4,64,256]{2,1,0:T(8,128)(2,1)}, bf16[4,64,256]{2,1,0:T(8,128)(2,1)}, bf16[4,64,256]{2,1,0:T(8,128)(2,1)}) custom-call(bf16[256,1024]{1,0:T(8,128)(2,1)} %copy-done.4, bf16[256,1024]{1,0:T(8,128)(2,1)} %bitcast.6, bf16[256,1024]{1,0:T(8,128)(2,1)} %copy-done.1, bf16[256,1024]{1,0:T(8,128)(2,1)} %copy-done.2, ...), custom_call_target="tpu_custom_call" | custom-call | flops 1073741824 | bytes 4718592 | tf_op jit(solution)/shard_map/pallas_call | solution.py:46
  37.3 0.0 copy-done
  37.3 0.7 collective-permute-start.10
  38.0 0.0 copy-start.19
  38.0 0.0 copy-start.3
  38.0 0.8 collective-permute-start.11
  38.8 4.7 %shard_map.28 = (bf16[6,64,256]{2,1,0:T(8,128)(2,1)}, bf16[6,64,256]{2,1,0:T(8,128)(2,1)}, bf16[6,64,256]{2,1,0:T(8,128)(2,1)}, bf16[6,64,256]{2,1,0:T(8,128)(2,1)}) custom-call(bf16[256,1024]{1,0:T(8,128)(2,1)} %copy-done.4, bf16[256,1024]{1,0:T(8,128)(2,1)} %bitcast.7, bf16[256,1024]{1,0:T(8,128)(2,1)} %copy-done.1, bf16[256,1024]{1,0:T(8,128)(2,1)} %copy-done.9, ...), custom_call_target="tpu_custom_call" | custom-call | flops 1610612736 | bytes 3932160 | tf_op jit(solution)/shard_map/pallas_call | solution.py:46
  43.5 0.7 collective-permute-start.4
  44.2 0.7 collective-permute-start.5
  44.9 0.0 collective-permute-done.10.refs_6_
  44.9 0.7 collective-permute-start.6
  45.6 0.0 collective-permute-done.11.refs_7_
  45.6 0.7 collective-permute-start.9
  46.3 0.0 collective-permute-done.9.refs_5_
  46.3 1.3 %collective-permute-start.18 = (bf16[256,1024]{1,0:T(8,128)(2,1)S(1)}, bf16[256,1024]{1,0:T(8,128)(2,1)S(1)}, u32[]{:S(2)}, u32[]{:S(2)}) collective-permute-start(bf16[256,1024]{1,0:T(8,128)(2,1)S(1)} %copy-done.3), channel_id=1, source_target_pairs={{2,0},{5,7},{10,8},{13,15},{18,16},{21,23},{26,24},{29,31}} | collective-permute-start | bytes 1572872 | tf_op jit(solution)/shard_map/ppermute | solution.py:151
  47.6 0.0 collective-permute-done.20.refs_9_
  47.6 0.0 copy-start.5
  47.7 0.7 collective-permute-start.21
  48.4 0.0 collective-permute-done.4.refs_1_
  48.4 0.0 copy-start.10
  48.4 0.0 collective-permute-done.5.refs_2_
  48.4 0.0 collective-permute-done.6.refs_3_
  48.5 0.6 copy-done.10
  49.0 0.1 copy-done.11
  49.1 0.1 copy-done.12
  49.2 2.3 %shard_map.30 = (bf16[4,64,256]{2,1,0:T(8,128)(2,1)}, bf16[4,64,256]{2,1,0:T(8,128)(2,1)}, bf16[4,64,256]{2,1,0:T(8,128)(2,1)}, bf16[4,64,256]{2,1,0:T(8,128)(2,1)}) custom-call(bf16[6,64,256]{2,1,0:T(8,128)(2,1)} %get-tuple-element.22.refs_0_, bf16[6,64,256]{2,1,0:T(8,128)(2,1)} %copy-done.10, bf16[6,64,256]{2,1,0:T(8,128)(2,1)} %copy-done.11, ...), custom_call_target="tpu_custom_call" | custom-call | flops 655360 | bytes 1835008 | tf_op jit(solution)/shard_map/pallas_call | solution.py:76
  51.5 1.3 %collective-permute-start.12 = (bf16[4,64,256]{2,1,0:T(8,128)(2,1)}, bf16[4,64,256]{2,1,0:T(8,128)(2,1)S(1)}, u32[]{:S(2)}, u32[]{:S(2)}) collective-permute-start(bf16[4,64,256]{2,1,0:T(8,128)(2,1)} %get-tuple-element.31), channel_id=1, source_target_pairs={{2,0},{5,7},{10,8},{13,15},{18,16},{21,23},{26,24},{29,31}} | collective-permute-start | bytes 393224 | tf_op jit(solution)/shard_map/ppermute | solution.py:151
  52.8 0.7 collective-permute-start.13
  53.4 0.7 collective-permute-start.14
  54.1 40.6 %collective-permute-done.12 = bf16[4,64,256]{2,1,0:T(8,128)(2,1)S(1)} collective-permute-done((bf16[4,64,256]{2,1,0:T(8,128)(2,1)}, bf16[4,64,256]{2,1,0:T(8,128)(2,1)S(1)}, u32[]{:S(2)}, u32[]{:S(2)}) %collective-permute-start.12) | collective-permute-done | bytes 131104 | tf_op jit(solution)/shard_map/ppermute | solution.py:151
  94.8 0.0 collective-permute-done.13
  94.8 0.0 collective-permute-done.14
  94.8 0.6 collective-permute-start.15
  95.4 1.5 %collective-permute-start.16 = (bf16[4,64,256]{2,1,0:T(8,128)(2,1)S(1)}, bf16[4,64,256]{2,1,0:T(8,128)(2,1)S(1)}, u32[]{:S(2)}, u32[]{:S(2)}) collective-permute-start(bf16[4,64,256]{2,1,0:T(8,128)(2,1)S(1)} %add_add_fusion.refs_0_), channel_id=1, source_target_pairs={{0,16},{2,18},{4,20},{6,22},{7,23},{5,21},{3,19},{1,17},{8,24},{10... | collective-permute-start | bytes 393224 | tf_op jit(solution)/shard_map/ppermute | solution.py:157
  97.0 1.4 %collective-permute-start.17 = (bf16[4,64,256]{2,1,0:T(8,128)(2,1)S(1)}, bf16[4,64,256]{2,1,0:T(8,128)(2,1)S(1)}, u32[]{:S(2)}, u32[]{:S(2)}) collective-permute-start(bf16[4,64,256]{2,1,0:T(8,128)(2,1)S(1)} %add_add_fusion.refs_0_), channel_id=1, source_target_pairs={{0,24},{2,26},{4,28},{6,30},{7,31},{5,29},{3,27},{1,25},{8,16},{10... | collective-permute-start | bytes 393224 | tf_op jit(solution)/shard_map/ppermute | solution.py:157
  98.4 1.5 %collective-permute-done.15.refs_1_ = bf16[4,64,256]{2,1,0:T(8,128)(2,1)S(1)} collective-permute-done((bf16[4,64,256]{2,1,0:T(8,128)(2,1)S(1)}, bf16[4,64,256]{2,1,0:T(8,128)(2,1)S(1)}, u32[]{:S(2)}, u32[]{:S(2)}) %collective-permute-start.15) | collective-permute-done | bytes 131104 | tf_op jit(solution)/shard_map/ppermute | solution.py:157
  99.9 0.5 collective-permute-done.16.refs_2_
  100.4 2.4 %collective-permute-done.17.refs_3_ = bf16[4,64,256]{2,1,0:T(8,128)(2,1)S(1)} collective-permute-done((bf16[4,64,256]{2,1,0:T(8,128)(2,1)S(1)}, bf16[4,64,256]{2,1,0:T(8,128)(2,1)S(1)}, u32[]{:S(2)}, u32[]{:S(2)}) %collective-permute-start.17) | collective-permute-done | bytes 131104 | tf_op jit(solution)/shard_map/ppermute | solution.py:157
  102.8 0.0 collective-permute-done.18.refs_7_
  102.8 0.0 collective-permute-done.21.refs_10_
  102.9 0.6 copy-done.18
  103.5 0.2 copy-done.6
  103.7 0.8 copy-done.7
  104.5 4.3 %shard_map.31 = bf16[256,1024]{1,0:T(8,128)(2,1)} custom-call(bf16[4,64,256]{2,1,0:T(8,128)(2,1)} %copy-done.8, bf16[4,64,256]{2,1,0:T(8,128)(2,1)} %copy-done.16, bf16[4,64,256]{2,1,0:T(8,128)(2,1)} %copy-done.17, bf16[4,64,256]{2,1,0:T(8,128)(2,1)} %copy-done.18, bf16[256,1024]{1,0:T(8,128)(2,1)} %bitcast.8, bf16[256,1024]{1,0:T(8,128)(2,1)} %copy-done.1, ...), custom_call_target="tpu_custom_call" | custom-call | flops 536870912 | bytes 4718592 | tf_op jit(solution)/shard_map/pallas_call | solution.py:121
  (26 shorter events, 0.1 us)
Async XLA Ops:
  0.0 12.3 %collective-permute-start = (bf16[256,1024]{1,0:T(8,128)(2,1)}, bf16[256,1024]{1,0:T(8,128)(2,1)S(1)}, u32[]{:S(2)}, u32[]{:S(2)}) collective-permute-start(bf16[256,1024]{1,0:T(8,128)(2,1)} %bitcast.3), channel_id=1, source_target_pairs={{2,0},{4,2},{6,4},{5,7},{3,5},{1,3},{10,8},{12,10},{14,12},{13,15}... | collective-permute-start | bytes 1572872 | tf_op jit(solution)/shard_map/ppermute | solution.py:151
  12.3 19.4 %copy-start.1 = (bf16[256,1024]{1,0:T(8,128)(2,1)}, bf16[256,1024]{1,0:T(8,128)(2,1)S(1)}, u32[]{:S(2)}) copy-start(bf16[256,1024]{1,0:T(8,128)(2,1)S(1)} %collective-permute-done.refs_2_.refs_5_) | copy-start | bytes 1572868
  12.3 10.9 %collective-permute-start.2 = (bf16[256,1024]{1,0:T(8,128)(2,1)}, bf16[256,1024]{1,0:T(8,128)(2,1)S(1)}, u32[]{:S(2)}, u32[]{:S(2)}) collective-permute-start(bf16[256,1024]{1,0:T(8,128)(2,1)} %bitcast.9), channel_id=1, source_target_pairs={{0,2},{7,5},{8,10},{15,13},{16,18},{23,21},{24,26},{31,29}} | collective-permute-start | bytes 1572872 | tf_op jit(solution)/shard_map/ppermute | solution.py:151
  16.3 11.5 %collective-permute-start.7 = (bf16[256,1024]{1,0:T(8,128)(2,1)S(1)}, bf16[256,1024]{1,0:T(8,128)(2,1)S(1)}, u32[]{:S(2)}, u32[]{:S(2)}) collective-permute-start(bf16[256,1024]{1,0:T(8,128)(2,1)S(1)} %collective-permute-done.refs_2_.refs_5_), channel_id=1, source_target_pairs={{2,0},{4,2},{5,7},{3,5},{10,8},{12,10},{13,15},{11,13},{18,16},{20... | collective-permute-start | bytes 1572872 | tf_op jit(solution)/shard_map/ppermute | solution.py:151
  17.6 13.9 %collective-permute-start.1 = (bf16[256,1024]{1,0:T(8,128)(2,1)}, bf16[256,1024]{1,0:T(8,128)(2,1)S(1)}, u32[]{:S(2)}, u32[]{:S(2)}) collective-permute-start(bf16[256,1024]{1,0:T(8,128)(2,1)} %bitcast.4), channel_id=1, source_target_pairs={{0,2},{7,5},{8,10},{15,13},{16,18},{23,21},{24,26},{31,29}} | collective-permute-start | bytes 1572872 | tf_op jit(solution)/shard_map/ppermute | solution.py:151
  23.2 9.7 %copy-start.9 = (bf16[256,1024]{1,0:T(8,128)(2,1)}, bf16[256,1024]{1,0:T(8,128)(2,1)S(1)}, u32[]{:S(2)}) copy-start(bf16[256,1024]{1,0:T(8,128)(2,1)S(1)} %collective-permute-done.2.refs_3_.refs_4_) | copy-start | bytes 1572868
  27.8 3.9 %copy-start.2 = (bf16[256,1024]{1,0:T(8,128)(2,1)}, bf16[256,1024]{1,0:T(8,128)(2,1)S(1)}, u32[]{:S(2)}) copy-start(bf16[256,1024]{1,0:T(8,128)(2,1)S(1)} %collective-permute-done.7.refs_3_.refs_6_) | copy-start | bytes 1572868
  27.8 3.7 %collective-permute-start.19 = (bf16[256,1024]{1,0:T(8,128)(2,1)}, bf16[256,1024]{1,0:T(8,128)(2,1)S(1)}, u32[]{:S(2)}, u32[]{:S(2)}) collective-permute-start(bf16[256,1024]{1,0:T(8,128)(2,1)} %bitcast.5), channel_id=1, source_target_pairs={{2,4},{4,6},{5,3},{3,1},{10,12},{12,14},{13,11},{11,9},{18,20},{20... | collective-permute-start | bytes 1572872 | tf_op jit(solution)/shard_map/ppermute | solution.py:151
  28.5 4.4 %collective-permute-start.3 = (bf16[256,1024]{1,0:T(8,128)(2,1)}, bf16[256,1024]{1,0:T(8,128)(2,1)}, u32[]{:S(2)}, u32[]{:S(2)}) collective-permute-start(bf16[256,1024]{1,0:T(8,128)(2,1)} %bitcast.10), channel_id=1, source_target_pairs={{4,2},{3,5},{12,10},{11,13},{20,18},{19,21},{28,26},{27,29}} | collective-permute-start | bytes 1572872 | tf_op jit(solution)/shard_map/ppermute | solution.py:151
  30.0 3.0 %collective-permute-start.8 = (bf16[256,1024]{1,0:T(8,128)(2,1)}, bf16[256,1024]{1,0:T(8,128)(2,1)}, u32[]{:S(2)}, u32[]{:S(2)}) collective-permute-start(bf16[256,1024]{1,0:T(8,128)(2,1)} %bitcast.11), channel_id=1, source_target_pairs={{6,2},{1,5},{14,10},{9,13},{22,18},{17,21},{30,26},{25,29}} | collective-permute-start | bytes 1572872 | tf_op jit(solution)/shard_map/ppermute | solution.py:151
  31.5 0.8 copy-start.4
  32.3 5.1 %copy-start = (bf16[256,1024]{1,0:T(8,128)(2,1)}, bf16[256,1024]{1,0:T(8,128)(2,1)S(1)}, u32[]{:S(2)}) copy-start(bf16[256,1024]{1,0:T(8,128)(2,1)S(1)} %add.20.refs_8_) | copy-start | bytes 1572868
  32.3 15.4 %collective-permute-start.20 = (bf16[256,1024]{1,0:T(8,128)(2,1)S(1)}, bf16[256,1024]{1,0:T(8,128)(2,1)S(1)}, u32[]{:S(2)}, u32[]{:S(2)}) collective-permute-start(bf16[256,1024]{1,0:T(8,128)(2,1)S(1)} %add.20.refs_8_), channel_id=1, source_target_pairs={{2,4},{4,6},{5,3},{3,1},{10,12},{12,14},{13,11},{11,9},{18,20},{20... | collective-permute-start | bytes 1572872 | tf_op jit(solution)/shard_map/ppermute | solution.py:151
  37.3 7.6 %collective-permute-start.10 = (bf16[4,64,256]{2,1,0:T(8,128)(2,1)}, bf16[4,64,256]{2,1,0:T(8,128)(2,1)S(1)}, u32[]{:S(2)}, u32[]{:S(2)}) collective-permute-start(bf16[4,64,256]{2,1,0:T(8,128)(2,1)} %get-tuple-element.28), channel_id=1, source_target_pairs={{2,18},{5,21},{10,26},{13,29},{18,2},{21,5},{26,10},{29,13}} | collective-permute-start | bytes 393224 | tf_op jit(solution)/shard_map/ppermute | solution.py:157
  38.0 7.6 %copy-start.19 = (bf16[4,64,256]{2,1,0:T(8,128)(2,1)S(1)}, bf16[4,64,256]{2,1,0:T(8,128)(2,1)}, u32[]{:S(2)}) copy-start(bf16[4,64,256]{2,1,0:T(8,128)(2,1)} %get-tuple-element.27) | copy-start | bytes 393220
  38.0 8.3 %copy-start.3 = (bf16[256,1024]{1,0:T(8,128)(2,1)S(1)}, bf16[256,1024]{1,0:T(8,128)(2,1)}, u32[]{:S(2)}) copy-start(bf16[256,1024]{1,0:T(8,128)(2,1)} %copy-done.2) | copy-start | bytes 1572868
  38.0 7.6 %collective-permute-start.11 = (bf16[4,64,256]{2,1,0:T(8,128)(2,1)}, bf16[4,64,256]{2,1,0:T(8,128)(2,1)S(1)}, u32[]{:S(2)}, u32[]{:S(2)}) collective-permute-start(bf16[4,64,256]{2,1,0:T(8,128)(2,1)} %get-tuple-element.29), channel_id=1, source_target_pairs={{2,26},{5,29},{10,18},{13,21},{18,10},{21,13},{26,2},{29,5}} | collective-permute-start | bytes 393224 | tf_op jit(solution)/shard_map/ppermute | solution.py:157
  43.5 4.8 %collective-permute-start.4 = (bf16[6,64,256]{2,1,0:T(8,128)(2,1)}, bf16[6,64,256]{2,1,0:T(8,128)(2,1)S(1)}, u32[]{:S(2)}, u32[]{:S(2)}) collective-permute-start(bf16[6,64,256]{2,1,0:T(8,128)(2,1)} %get-tuple-element.23), channel_id=1, source_target_pairs={{2,10},{5,13},{10,2},{13,5},{18,26},{21,29},{26,18},{29,21}} | collective-permute-start | bytes 589832 | tf_op jit(solution)/shard_map/ppermute | solution.py:157
  44.2 4.2 %collective-permute-start.5 = (bf16[6,64,256]{2,1,0:T(8,128)(2,1)}, bf16[6,64,256]{2,1,0:T(8,128)(2,1)S(1)}, u32[]{:S(2)}, u32[]{:S(2)}) collective-permute-start(bf16[6,64,256]{2,1,0:T(8,128)(2,1)} %get-tuple-element.24), channel_id=1, source_target_pairs={{2,18},{5,21},{10,26},{13,29},{18,2},{21,5},{26,10},{29,13}} | collective-permute-start | bytes 589832 | tf_op jit(solution)/shard_map/ppermute | solution.py:157
  44.9 3.5 %copy-start.13 = (bf16[4,64,256]{2,1,0:T(8,128)(2,1)}, bf16[4,64,256]{2,1,0:T(8,128)(2,1)S(1)}, u32[]{:S(2)}) copy-start(bf16[4,64,256]{2,1,0:T(8,128)(2,1)S(1)} %collective-permute-done.10.refs_6_) | copy-start | bytes 393220
  44.9 3.5 %collective-permute-start.6 = (bf16[6,64,256]{2,1,0:T(8,128)(2,1)}, bf16[6,64,256]{2,1,0:T(8,128)(2,1)S(1)}, u32[]{:S(2)}, u32[]{:S(2)}) collective-permute-start(bf16[6,64,256]{2,1,0:T(8,128)(2,1)} %get-tuple-element.25), channel_id=1, source_target_pairs={{2,26},{5,29},{10,18},{13,21},{18,10},{21,13},{26,2},{29,5}} | collective-permute-start | bytes 589832 | tf_op jit(solution)/shard_map/ppermute | solution.py:157
  45.6 2.8 %copy-start.14 = (bf16[4,64,256]{2,1,0:T(8,128)(2,1)}, bf16[4,64,256]{2,1,0:T(8,128)(2,1)S(1)}, u32[]{:S(2)}) copy-start(bf16[4,64,256]{2,1,0:T(8,128)(2,1)S(1)} %collective-permute-done.11.refs_7_) | copy-start | bytes 393220
  45.6 0.7 collective-permute-start.9
  46.3 2.1 %copy-start.15 = (bf16[4,64,256]{2,1,0:T(8,128)(2,1)}, bf16[4,64,256]{2,1,0:T(8,128)(2,1)S(1)}, u32[]{:S(2)}) copy-start(bf16[4,64,256]{2,1,0:T(8,128)(2,1)S(1)} %collective-permute-done.9.refs_5_) | copy-start | bytes 393220
  46.3 56.5 %collective-permute-start.18 = (bf16[256,1024]{1,0:T(8,128)(2,1)S(1)}, bf16[256,1024]{1,0:T(8,128)(2,1)S(1)}, u32[]{:S(2)}, u32[]{:S(2)}) collective-permute-start(bf16[256,1024]{1,0:T(8,128)(2,1)S(1)} %copy-done.3), channel_id=1, source_target_pairs={{2,0},{5,7},{10,8},{13,15},{18,16},{21,23},{26,24},{29,31}} | collective-permute-start | bytes 1572872 | tf_op jit(solution)/shard_map/ppermute | solution.py:151
  47.6 3.8 %copy-start.5 = (bf16[256,1024]{1,0:T(8,128)(2,1)}, bf16[256,1024]{1,0:T(8,128)(2,1)S(1)}, u32[]{:S(2)}) copy-start(bf16[256,1024]{1,0:T(8,128)(2,1)S(1)} %collective-permute-done.20.refs_9_) | copy-start | bytes 1572868
  47.7 55.2 %collective-permute-start.21 = (bf16[256,1024]{1,0:T(8,128)(2,1)S(1)}, bf16[256,1024]{1,0:T(8,128)(2,1)S(1)}, u32[]{:S(2)}, u32[]{:S(2)}) collective-permute-start(bf16[256,1024]{1,0:T(8,128)(2,1)S(1)} %collective-permute-done.20.refs_9_), channel_id=1, source_target_pairs={{4,6},{3,1},{12,14},{11,9},{20,22},{19,17},{28,30},{27,25}} | collective-permute-start | bytes 1572872 | tf_op jit(solution)/shard_map/ppermute | solution.py:151
  48.4 0.7 copy-start.10
  48.4 0.7 copy-start.11
  48.4 0.8 copy-start.12
  51.5 43.3 %collective-permute-start.12 = (bf16[4,64,256]{2,1,0:T(8,128)(2,1)}, bf16[4,64,256]{2,1,0:T(8,128)(2,1)S(1)}, u32[]{:S(2)}, u32[]{:S(2)}) collective-permute-start(bf16[4,64,256]{2,1,0:T(8,128)(2,1)} %get-tuple-element.31), channel_id=1, source_target_pairs={{2,0},{5,7},{10,8},{13,15},{18,16},{21,23},{26,24},{29,31}} | collective-permute-start | bytes 393224 | tf_op jit(solution)/shard_map/ppermute | solution.py:151
  52.8 42.0 %collective-permute-start.13 = (bf16[4,64,256]{2,1,0:T(8,128)(2,1)}, bf16[4,64,256]{2,1,0:T(8,128)(2,1)S(1)}, u32[]{:S(2)}, u32[]{:S(2)}) collective-permute-start(bf16[4,64,256]{2,1,0:T(8,128)(2,1)} %get-tuple-element.32), channel_id=1, source_target_pairs={{2,4},{5,3},{10,12},{13,11},{18,20},{21,19},{26,28},{29,27}} | collective-permute-start | bytes 393224 | tf_op jit(solution)/shard_map/ppermute | solution.py:151
  53.4 41.3 %collective-permute-start.14 = (bf16[4,64,256]{2,1,0:T(8,128)(2,1)}, bf16[4,64,256]{2,1,0:T(8,128)(2,1)S(1)}, u32[]{:S(2)}, u32[]{:S(2)}) collective-permute-start(bf16[4,64,256]{2,1,0:T(8,128)(2,1)} %get-tuple-element.33), channel_id=1, source_target_pairs={{2,6},{5,1},{10,14},{13,9},{18,22},{21,17},{26,30},{29,25}} | collective-permute-start | bytes 393224 | tf_op jit(solution)/shard_map/ppermute | solution.py:151
  94.8 8.0 %copy-start.8 = (bf16[4,64,256]{2,1,0:T(8,128)(2,1)}, bf16[4,64,256]{2,1,0:T(8,128)(2,1)S(1)}, u32[]{:S(2)}) copy-start(bf16[4,64,256]{2,1,0:T(8,128)(2,1)S(1)} %add_add_fusion.refs_0_) | copy-start | bytes 393220
  94.8 5.0 %collective-permute-start.15 = (bf16[4,64,256]{2,1,0:T(8,128)(2,1)S(1)}, bf16[4,64,256]{2,1,0:T(8,128)(2,1)S(1)}, u32[]{:S(2)}, u32[]{:S(2)}) collective-permute-start(bf16[4,64,256]{2,1,0:T(8,128)(2,1)S(1)} %add_add_fusion.refs_0_), channel_id=1, source_target_pairs={{0,8},{2,10},{4,12},{6,14},{7,15},{5,13},{3,11},{1,9},{8,0},{10,2}... | collective-permute-start | bytes 393224 | tf_op jit(solution)/shard_map/ppermute | solution.py:157
  95.4 5.0 %collective-permute-start.16 = (bf16[4,64,256]{2,1,0:T(8,128)(2,1)S(1)}, bf16[4,64,256]{2,1,0:T(8,128)(2,1)S(1)}, u32[]{:S(2)}, u32[]{:S(2)}) collective-permute-start(bf16[4,64,256]{2,1,0:T(8,128)(2,1)S(1)} %add_add_fusion.refs_0_), channel_id=1, source_target_pairs={{0,16},{2,18},{4,20},{6,22},{7,23},{5,21},{3,19},{1,17},{8,24},{10... | collective-permute-start | bytes 393224 | tf_op jit(solution)/shard_map/ppermute | solution.py:157
  97.0 5.9 %collective-permute-start.17 = (bf16[4,64,256]{2,1,0:T(8,128)(2,1)S(1)}, bf16[4,64,256]{2,1,0:T(8,128)(2,1)S(1)}, u32[]{:S(2)}, u32[]{:S(2)}) collective-permute-start(bf16[4,64,256]{2,1,0:T(8,128)(2,1)S(1)} %add_add_fusion.refs_0_), channel_id=1, source_target_pairs={{0,24},{2,26},{4,28},{6,30},{7,31},{5,29},{3,27},{1,25},{8,16},{10... | collective-permute-start | bytes 393224 | tf_op jit(solution)/shard_map/ppermute | solution.py:157
  99.9 3.0 %copy-start.16 = (bf16[4,64,256]{2,1,0:T(8,128)(2,1)}, bf16[4,64,256]{2,1,0:T(8,128)(2,1)S(1)}, u32[]{:S(2)}) copy-start(bf16[4,64,256]{2,1,0:T(8,128)(2,1)S(1)} %collective-permute-done.15.refs_1_) | copy-start | bytes 393220
  100.4 2.5 %copy-start.17 = (bf16[4,64,256]{2,1,0:T(8,128)(2,1)}, bf16[4,64,256]{2,1,0:T(8,128)(2,1)S(1)}, u32[]{:S(2)}) copy-start(bf16[4,64,256]{2,1,0:T(8,128)(2,1)S(1)} %collective-permute-done.16.refs_2_) | copy-start | bytes 393220
  102.8 0.6 copy-start.18
  102.8 0.8 copy-start.6
  103.7 0.8 copy-start.7
